TPU v7x, 256 devices: a whole 4x4x8 slice. The times are simulated.
256 devices in a mesh: expert: 32 (over y, x, core), group: 8 (over z).
Axes of the slice: x: 4, y: 4, z: 8, core: 2. Of those that a mesh axis runs over, the one named last changes fastest.
Arguments:
- activations: bfloat16 [4096, 7168], P('expert', 'group'), may hold values from -6 to 6
- out_grads: bfloat16 [4096, 7168], P('expert', 'group'), may hold values from -6 to 6
- sketch_op: bfloat16 [7168, 128], P('group'), may hold values from -0.0625 to 0.0625
- block_lists: int32 [256, 32], P('expert'), may hold values from 0 to 31, as said below
- block_counts: int32 [256], P('expert'), may hold values from 1 to 32
- gate_values: bfloat16 [256, 32, 128], P('expert'), may hold values from 0.05 to 9, as said below
Outputs:
- basis_out: float32 [256, 7168, 128], P('expert', 'group')
Inputs may be any that keep to these rules, and one draw needn't show every extreme that they name: `block_lists`: each row is an ordering of all 32 block numbers, each once. `gate_values`: positive.
All inputs are finite; a program needn't handle non-finite values.
Results may differ from a plain program's by a relative error of at most 0.0042.
The roundings to bfloat16 on the way count: a program that leaves them out, or rounds other values in their place, can miss the bound.
Values may be sent and summed in bfloat16 or wider, within the bound.
No kernel may reach another device: no remote copies, remote signals or barrier semaphores. Data moves between devices by JAX's collectives and lax.ppermute only.
A program may use at most 64 MiB of HBM per device.

v0:
```python
import math
import jax
import jax.numpy as jnp
from jax import lax
from jax.sharding import PartitionSpec as P


def sketch_rows(rows_x, rows_y, weight_part):
    count_exp = weight_part.shape[0]
    row_count = rows_x.shape[0]
    sketch_rank = rows_y.shape[1]
    rows_wide = rows_y.astype(jnp.float32)
    contract = (((0,), (0,)), ((), ()))
    scaled = (weight_part.T[:, :, None] * rows_wide[:, None, :]).astype(jnp.bfloat16)
    scaled = scaled.reshape(row_count, count_exp * sketch_rank)
    return lax.dot_general(rows_x, scaled, contract, preferred_element_type=jnp.float32)


def gram_of(sketch_flat, sketch_rank):
    shaped = sketch_flat.reshape(sketch_flat.shape[0], -1, sketch_rank)
    return jnp.einsum("dkr,dks->rs", shaped, shaped, precision=lax.Precision.HIGHEST)


def on_device(activations, out_grads, sketch_op, block_lists, block_counts, gate_values):
    sketch_rank = sketch_op.shape[1]
    feat_width = activations.shape[1]
    local_exp = block_lists.shape[0]
    blocks = block_lists.shape[1]
    partial_sketch = jnp.dot(out_grads, sketch_op, preferred_element_type=jnp.float32)
    sketched = lax.psum(partial_sketch, "group").astype(jnp.bfloat16)
    slot_ids = jnp.arange(blocks, dtype=jnp.int32)
    slot_live = slot_ids[None, :] < block_counts[:, None]
    onehot = ((block_lists[:, :, None] == slot_ids[None, None, :]) & slot_live[:, :, None]).astype(
        jnp.float32
    )
    weights = jnp.einsum("ejb,ejt->ebt", onehot, gate_values.astype(jnp.float32)).reshape(
        local_exp, -1
    )
    piece_rows = lax.all_gather(activations, "expert", axis=0, tiled=True)
    piece_sketch = lax.all_gather(sketched, "expert", axis=0, tiled=True)
    sketch_all = sketch_rows(piece_rows, piece_sketch, weights)
    gram_total = lax.psum(gram_of(sketch_all, sketch_rank), ("expert", "group"))
    factor = jnp.linalg.cholesky(gram_total)
    stacked = (
        sketch_all.reshape(feat_width, local_exp, sketch_rank)
        .transpose(1, 0, 2)
        .reshape(-1, sketch_rank)
    )
    basis_flat = lax.linalg.triangular_solve(
        factor, stacked, left_side=False, lower=True, transpose_a=True
    )
    out_scale = math.sqrt(local_exp * lax.axis_size("expert") * feat_width * lax.axis_size("group"))
    return (basis_flat * out_scale).reshape(local_exp, feat_width, sketch_rank)


def solution(mesh):
    in_specs = (
        P("expert", "group"),
        P("expert", "group"),
        P("group", None),
        P("expert", None),
        P("expert"),
        P("expert", None, None),
    )
    out_specs = P("expert", "group", None)
    return jax.shard_map(
        on_device, mesh=mesh, in_specs=in_specs, out_specs=out_specs, check_vma=False
    )
```

profile of v0, /device:TPU:1, one launch (start us, length us, event | category | flops | bytes accessed | tf_op | source)
XLA Modules:
  0.0 443.5 jit_solution(5734964180359648877)
XLA Ops:
  6.5 0.9 copy-done
  7.5 1.1 fusion.10
  8.6 27.5 %psum.14 = bf16[128,128]{1,0:T(8,128)(2,1)} all-reduce(f32[128,128]{1,0:T(8,128)S(1)} %fusion.10), channel_id=1, replica_groups=mesh['expert'=32,'group'=8] {'group'}, use_global_device_ids=true, to_apply=%region_0.0 | all-reduce | flops 16384 | bytes 98304 | tf_op jit(solution)/shard_map/psum | solution.py:30
  36.2 0.7 all-gather.5.cloned.1.call-update
  37.0 0.7 iota_compare_fusion.3
  37.7 1.0 convolution_bitcast_fusion
  38.7 0.1 copy.26
  38.8 0.6 copy.11
  39.4 50.1 %all-gather.3.cloned.1.call-done = bf16[4096,128]{1,0:T(8,128)(2,1)} async-done(((bf16[128,128]{1,0:T(8,128)(2,1)}), bf16[4096,128]{1,0:T(8,128)(2,1)}) %all-gather.3.cloned.1.call-update) | async-done | bytes 1048592 | tf_op jit(solution)/shard_map/all_gather | solution.py:40
  89.5 1.4 convert_element_type.16
  90.9 16.4 %multiply_convert_fusion = bf16[4096,8,128]{2,1,0:T(8,128)(2,1)} fusion(f32[4096,128]{1,0:T(8,128)S(1)} %convert_element_type.16, f32[4096,8]{1,0:T(8,128)S(1)} %copy.11), kind=kLoop, calls=%fused_computation | loop fusion | flops 8388608 | bytes 10616832 | tf_op jit(solution)/shard_map/convert_element_type | solution.py:14
  107.2 40.0 %all-gather.5.cloned.1.call-done = bf16[4096,896]{1,0:T(8,128)(2,1)} async-done(((bf16[128,896]{1,0:T(8,128)(2,1)}), bf16[4096,896]{1,0:T(8,128)(2,1)}) %all-gather.5.cloned.1.call-update) | async-done | bytes 7340048 | tf_op jit(solution)/shard_map/all_gather | solution.py:39
  147.3 12.9 %fusion = f32[1024,896]{1,0:T(8,128)S(1)} fusion(bf16[4096,896]{1,0:T(8,128)(2,1)} %all-gather.5.cloned.1.call-done, bf16[512,8,8,128]{3,2,1,0:T(8,128)(2,1)} %bitcast.40), kind=kOutput, calls=%fused_computation.2 | convolution fusion | flops 7516192768 | bytes 19398656 | tf_op jit(solution)/shard_map/dot_general | solution.py:16
  160.2 1.8 copy-done.1
  162.1 3.6 convolution_bitcast_fusion.1
  165.7 5.0 %copy.12 = f32[896,8,128]{2,0,1:T(8,128)} copy(f32[896,8,128]{0,2,1:T(8,128)} %bitcast.38) | data formatting | bytes 7340032 | tf_op jit(solution)/shard_map/reshape | solution.py:45
  170.7 235.7 %all-reduce.2.cloned.1.call-done = f32[128,128]{0,1:T(8,128)} async-done(((f32[128,128]{0,1:T(8,128)}), f32[128,128]{0,1:T(8,128)}) %all-reduce.2.cloned.1.call-update) | async-done | bytes 65552 | tf_op jit(solution)/shard_map/psum | solution.py:42
  406.4 0.9 copy.15
  407.4 0.9 fusion.7
  408.2 11.7 %cholesky.16 = f32[128,128]{1,0:T(8,128)S(1)} custom-call(f32[128,128]{1,0:T(8,128)S(1)} %fusion.7), custom_call_target="Cholesky" | custom-call | tf_op jit(solution)/shard_map/jit(cholesky)/cholesky | solution.py:43
  420.0 0.6 compare_reduce_fusion
  420.6 0.7 fusion.5
  421.3 9.8 %custom-call.6 = f32[1,128,128]{1,2,0:T(8,128)S(1)} custom-call(f32[1,128,128]{2,1,0:T(8,128)S(1)} %fusion.5), custom_call_target="InvertDiagBlocksLowerTriangular" | custom-call | tf_op jit(solution)/shard_map/triangular_solve | solution.py:49
  431.1 5.9 %convolution_multiply_fusion = f32[7168,128]{1,0:T(8,128)} fusion(f32[7168,128]{1,0:T(8,128)} %bitcast.39, f32[1,128,128]{1,2,0:T(8,128)S(1)} %custom-call.6), kind=kOutput, calls=%fused_computation.1 | convolution fusion | flops 1410203648 | bytes 7405568 | tf_op jit(solution)/shard_map/triangular_solve | solution.py:49
  (8 shorter events, 0.2 us)
Async XLA Ops:
  6.5 0.9 copy-start
  6.5 83.0 %all-gather.3.cloned.1.call-start = ((), (), s32[]{:S(2)}) async-start(), calls=%async_computation | async-start | bytes 1081344 | tf_op jit(solution)/shard_map/all_gather | solution.py:40
  36.2 111.1 %all-gather.5.cloned.1.call-start = ((), (), s32[]{:S(2)}) async-start(), calls=%async_computation.1 | async-start | bytes 7569408 | tf_op jit(solution)/shard_map/all_gather | solution.py:39
  36.9 369.5 %all-reduce.2.cloned.1.call-start = ((), (), s32[]{:S(2)}) async-start(), calls=%async_computation.2 | async-start | bytes 131072 | tf_op jit(solution)/shard_map/psum | solution.py:42
  160.2 1.8 copy-start.1
Sparse Core Ops, SparseCore 0:
  36.3 53.1 all-gather.2
  92.0 55.1 all-gather.4
  165.8 240.5 all-reduce.1
where the time goes:
time: 444 us
  waiting for transfers between devices  327 us (74%)
  other arithmetic  42.2 us (10%)
  blocking collectives  27.5 us (6%)
  matrix products  24.7 us (6%)
  between operations  13.2 us (3%)
  local copies, waits for them, and re-layouts  9.39 us (2%)
    psum x1, waiting for transfers between devices, on_device(): gram_total = lax.psum(gram_of(sketch_all, sketch_rank), ('expert', 'group'))  236 us
    all_gather x1, waiting for transfers between devices, on_device(): piece_sketch = lax.all_gather(sketched, 'expert', axis=0, tiled=True)  50.1 us
    all_gather x1, waiting for transfers between devices, on_device(): piece_rows = lax.all_gather(activations, 'expert', axis=0, tiled=True)  40 us
    psum x1, blocking collectives, on_device(): sketched = lax.psum(partial_sketch, 'group').astype(jnp.bfloat16)  27.5 us
    convert_element_type x1, other arithmetic, sketch_rows(): (weight_part.T[:, :, None] * rows_wide[:, None, :]).astype(jnp.bfloat16)  16.4 us
    dot_general x1, matrix products, sketch_rows(): lax.dot_general(rows_x, scaled, contract, preferred_element_type=jnp.floa...  12.9 us
    another operation x3, other arithmetic, on_device(): factor = jnp.linalg.cholesky(gram_total)  12.4 us
    another operation x2, other arithmetic, on_device(): lax.linalg.triangular_solve(factor, stacked, left_side=False, lower=True,...  10.5 us
  transfers between devices with their start and end apart: 3, of which 3 were waited for; matrix products, arithmetic and copies ran while one was open for 6% of the time, Pallas kernels for 0%

commit v1 on v0

--- a/solution.py
+++ b/solution.py
@@ -37,7 +37,8 @@
         local_exp, -1
     )
     piece_rows = lax.all_gather(activations, "expert", axis=0, tiled=True)
-    piece_sketch = lax.all_gather(sketched, "expert", axis=0, tiled=True)
+    sent = jnp.stack([sketched] * lax.axis_size("expert"))
+    piece_sketch = jnp.concatenate(lax.all_to_all(sent, "expert", 0, 0), axis=0)
     sketch_all = sketch_rows(piece_rows, piece_sketch, weights)
     gram_total = lax.psum(gram_of(sketch_all, sketch_rank), ("expert", "group"))
     factor = jnp.linalg.cholesky(gram_total)

time: 444 us -> 389 us (0.88)
  waiting for transfers between devices: 327 us -> 259 us
  starting transfers between devices: 0.08 us -> 14.1 us
    all_gather x1 -> x0, waiting for transfers between devices: 50.1 us -> none  [on_device(): piece_sketch = lax.all_gather(sketched, 'expert', axis=0, tiled=True)]
    all_gather x1, waiting for transfers between devices: 40 us -> 0.01 us  [on_device(): piece_rows = lax.all_gather(activations, 'expert', axis=0, tiled=True)]
    all_to_all x0 -> x1, waiting for transfers between devices: none -> 25.3 us  [on_device(): piece_sketch = jnp.concatenate(lax.all_to_all(sent, 'expert', 0, 0), axis=0)]
    all_to_all x0 -> x1, starting transfers between devices: none -> 14 us  [on_device(): piece_sketch = jnp.concatenate(lax.all_to_all(sent, 'expert', 0, 0), axis=0)]
  transfers between devices with their start and end apart: 3 -> 3, of which waited for: 3 -> 2; matrix products, arithmetic and copies ran while one was open for 6% -> 6% of each run, Pallas kernels for 0% -> 0%
where the time goes in v1:
time: 389 us; the launch traced here: 388 us
  waiting for transfers between devices  259 us (67%)
  other arithmetic  40.4 us (10%)
  blocking collectives  27.8 us (7%)
  matrix products  23.8 us (6%)
  starting transfers between devices  14.1 us (4%)
  between operations  13.5 us (3%)
  local copies, waits for them, and re-layouts  9.87 us (3%)
    psum x1, waiting for transfers between devices, on_device(): gram_total = lax.psum(gram_of(sketch_all, sketch_rank), ('expert', 'group'))  233 us
    psum x1, blocking collectives, on_device(): sketched = lax.psum(partial_sketch, 'group').astype(jnp.bfloat16)  27.8 us
    all_to_all x1, waiting for transfers between devices, on_device(): piece_sketch = jnp.concatenate(lax.all_to_all(sent, 'expert', 0, 0), axis=0)  25.3 us
    convert_element_type x1, other arithmetic, sketch_rows(): (weight_part.T[:, :, None] * rows_wide[:, None, :]).astype(jnp.bfloat16)  16.4 us
    all_to_all x1, starting transfers between devices, on_device(): piece_sketch = jnp.concatenate(lax.all_to_all(sent, 'expert', 0, 0), axis=0)  14 us
    dot_general x1, matrix products, sketch_rows(): lax.dot_general(rows_x, scaled, contract, preferred_element_type=jnp.floa...  13 us
    another operation x3, other arithmetic, on_device(): factor = jnp.linalg.cholesky(gram_total)  12.4 us
    another operation x2, other arithmetic, on_device(): lax.linalg.triangular_solve(factor, stacked, left_side=False, lower=True,...  10.5 us
  transfers between devices with their start and end apart: 3, of which 2 were waited for; matrix products, arithmetic and copies ran while one was open for 6% of the time, Pallas kernels for 0%

profile of v1, /device:TPU:1, one launch (start us, length us, event | category | flops | bytes accessed | tf_op | source)
XLA Modules:
  0.0 388.5 jit_solution(4507928852008643385)
XLA Ops:
  6.6 0.7 all-gather.2.cloned.1.call-update
  7.3 0.2 copy-done
  7.5 1.1 fusion.10
  8.6 27.8 %psum.14 = bf16[128,128]{1,0:T(8,128)(2,1)S(1)} all-reduce(f32[128,128]{1,0:T(8,128)S(1)} %fusion.10), channel_id=1, replica_groups=mesh['expert'=32,'group'=8] {'group'}, use_global_device_ids=true, to_apply=%region_0.0 | all-reduce | flops 16384 | bytes 98304 | tf_op jit(solution)/shard_map/psum | solution.py:30
  36.4 1.2 stack.2
  37.6 14.0 %all-to-all-start = ((bf16[32,128,128]{2,1,0:T(8,128)(2,1)}), bf16[32,128,128]{2,1,0:T(8,128)(2,1)S(1)}, u32[]{:S(2)}, u32[]{:S(2)}) async-start(bf16[32,128,128]{2,1,0:T(8,128)(2,1)} %stack.2), calls=%async_computation | async-start | bytes 2097152 | tf_op jit(solution)/shard_map/all_to_all | solution.py:41
  51.8 0.1 convolution_bitcast_fusion
  51.9 0.1 copy.26
  52.0 0.6 copy.11
  52.6 25.3 %all-to-all-done = bf16[32,128,128]{2,1,0:T(8,128)(2,1)S(1)} async-done(((bf16[32,128,128]{2,1,0:T(8,128)(2,1)}), bf16[32,128,128]{2,1,0:T(8,128)(2,1)S(1)}, u32[]{:S(2)}, u32[]{:S(2)}) %all-to-all-start) | async-done | bytes 1048608 | tf_op jit(solution)/shard_map/all_to_all | solution.py:41
  77.9 0.2 bitcast_convert_fusion
  78.1 16.4 %multiply_convert_fusion = bf16[4096,8,128]{2,1,0:T(8,128)(2,1)} fusion(f32[4096,128]{1,0:T(8,128)S(1)} %bitcast_convert_fusion, f32[4096,8]{1,0:T(8,128)S(1)} %copy.11), kind=kLoop, calls=%fused_computation | loop fusion | flops 8388608 | bytes 10616832 | tf_op jit(solution)/shard_map/convert_element_type | solution.py:14
  94.5 13.0 %fusion = f32[1024,896]{1,0:T(8,128)S(1)} fusion(bf16[4096,896]{1,0:T(8,128)(2,1)} %all-gather.2.cloned.1.call-done, bf16[512,8,8,128]{3,2,1,0:T(8,128)(2,1)} %bitcast.43), kind=kOutput, calls=%fused_computation.2 | convolution fusion | flops 7516192768 | bytes 19398656 | tf_op jit(solution)/shard_map/dot_general | solution.py:16
  107.4 1.8 copy-done.1
  109.3 3.6 convolution_bitcast_fusion.1
  112.9 5.0 %copy.12 = f32[896,8,128]{2,0,1:T(8,128)} copy(f32[896,8,128]{0,2,1:T(8,128)} %bitcast.41) | data formatting | bytes 7340032 | tf_op jit(solution)/shard_map/reshape | solution.py:46
  117.9 233.1 %all-reduce.2.cloned.1.call-done = f32[128,128]{0,1:T(8,128)} async-done(((f32[128,128]{0,1:T(8,128)}), f32[128,128]{0,1:T(8,128)}) %all-reduce.2.cloned.1.call-update) | async-done | bytes 65552 | tf_op jit(solution)/shard_map/psum | solution.py:43
  351.1 0.9 copy.15
  352.0 0.9 fusion.7
  352.9 11.7 %cholesky.16 = f32[128,128]{1,0:T(8,128)S(1)} custom-call(f32[128,128]{1,0:T(8,128)S(1)} %fusion.7), custom_call_target="Cholesky" | custom-call | tf_op jit(solution)/shard_map/jit(cholesky)/cholesky | solution.py:44
  364.6 0.6 compare_reduce_fusion
  365.3 0.7 fusion.5
  365.9 9.8 %custom-call.6 = f32[1,128,128]{1,2,0:T(8,128)S(1)} custom-call(f32[1,128,128]{2,1,0:T(8,128)S(1)} %fusion.5), custom_call_target="InvertDiagBlocksLowerTriangular" | custom-call | tf_op jit(solution)/shard_map/triangular_solve | solution.py:50
  375.7 5.9 %convolution_multiply_fusion = f32[7168,128]{1,0:T(8,128)} fusion(f32[7168,128]{1,0:T(8,128)} %bitcast.42, f32[1,128,128]{1,2,0:T(8,128)S(1)} %custom-call.6), kind=kOutput, calls=%fused_computation.1 | convolution fusion | flops 1410203648 | bytes 7405568 | tf_op jit(solution)/shard_map/triangular_solve | solution.py:50
  (14 shorter events, 0.2 us)
Async XLA Ops:
  6.5 0.9 copy-start
  6.5 45.1 %copy-start.4 = (s32[8]{0:T(128)S(1)}, s32[8]{0:T(128)}, u32[]{:S(2)}) copy-start(s32[8]{0:T(128)} %param.10) | copy-start | bytes 100
  6.5 45.2 %copy-start.2 = (bf16[8,32,128]{2,1,0:T(8,128)(2,1)S(1)}, bf16[8,32,128]{2,1,0:T(8,128)(2,1)}, u32[]{:S(2)}) copy-start(bf16[8,32,128]{2,1,0:T(8,128)(2,1)} %param.11) | copy-start | bytes 196612
  6.5 45.2 %copy-start.3 = (s32[8,32]{1,0:T(8,128)S(1)}, s32[8,32]{1,0:T(8,128)}, u32[]{:S(2)}) copy-start(s32[8,32]{1,0:T(8,128)} %param.9) | copy-start | bytes 3076
  6.5 87.9 %all-gather.2.cloned.1.call-start = ((), (), s32[]{:S(2)}) async-start(), calls=%async_computation.1 | async-start | bytes 7569408 | tf_op jit(solution)/shard_map/all_gather | solution.py:39
  37.6 40.3 %all-to-all-start = ((bf16[32,128,128]{2,1,0:T(8,128)(2,1)}), bf16[32,128,128]{2,1,0:T(8,128)(2,1)S(1)}, u32[]{:S(2)}, u32[]{:S(2)}) async-start(bf16[32,128,128]{2,1,0:T(8,128)(2,1)} %stack.2), calls=%async_computation | async-start | bytes 2097152 | tf_op jit(solution)/shard_map/all_to_all | solution.py:41
  51.6 299.4 %all-reduce.2.cloned.1.call-start = ((), (), s32[]{:S(2)}) async-start(), calls=%async_computation.2 | async-start | bytes 131072 | tf_op jit(solution)/shard_map/psum | solution.py:43
  107.4 1.8 copy-start.1
Sparse Core Ops, SparseCore 0:
  9.9 70.5 all-gather.1
  113.1 237.9 all-reduce.1
